TPU v7x, 128 devices: a whole 4x4x4 slice. The times are simulated.
128 devices in a mesh: nodes: 32 (over x, z, core), feat: 4 (over y).
Axes of the slice: x: 4, y: 4, z: 4, core: 2. Of those that a mesh axis runs over, the one named last changes fastest.
Arguments:
- features: bfloat16 [262144, 256], P('nodes', 'feat'), may hold values from -6 to 6
- weight: bfloat16 [256, 256], P(None, 'feat'), may hold values from -0.375 to 0.375
- adj_tiles: bfloat16 [12288, 128, 128], P('nodes'), may hold values from -0.21875 to 0.21875
- tile_row: int32 [12288], P('nodes'), may hold values from 0 to 63, as said below
- tile_col: int32 [12288], P('nodes'), may hold values from 0 to 2047, as said below
- cotangent: bfloat16 [262144, 256], P('nodes', 'feat'), may hold values from -6 to 6
Outputs:
- activated: bfloat16 [262144, 256], P('nodes', 'feat')
- grad_features: bfloat16 [262144, 256], P('nodes', 'feat')
- grad_weight: float32 [256, 256], P(None, 'feat')
Inputs may be any that keep to these rules, and one draw needn't show every extreme that they name: `tile_row`: tile k * 384 + s with s < 64 has block row s. Every device has at least one tile in each of its block rows. `tile_col`: tile k * 384 + s with s < 64 has column block k * 64 + s, the diagonal tile. Of a device's tiles, at most 2 have their column block on any one other device, and exactly 2 on its successor (k + 1) mod 32.
All inputs are finite; a program needn't handle non-finite values.
Results may differ from a plain program's by a relative error of at most 0.0061.
Values may be sent and summed in bfloat16 or wider, within the bound.
A program may use at most 192 MiB of HBM per device.

v0:
```python
import math

import jax
import jax.numpy as jnp
from jax import lax
from jax.sharding import PartitionSpec as P

CAP = 2


def per_device(features, weight, adj_tiles, tile_row, tile_col, cotangent):
    highest = lax.Precision.HIGHEST
    block_size = adj_tiles.shape[1]
    node_rows = features.shape[0]
    blocks_here = node_rows // block_size
    col_width = features.shape[1]
    slot_count = adj_tiles.shape[0]
    node_count = lax.axis_size("nodes")
    own_index = lax.axis_index("nodes")
    block_ids = jnp.arange(blocks_here, dtype=jnp.int32)
    full_rows = lax.all_gather(features, "feat", axis=1, tiled=True)
    proj = jnp.dot(full_rows, weight, preferred_element_type=jnp.float32).astype(jnp.bfloat16)
    owners = tile_col // blocks_here
    local_block = tile_col - owners * blocks_here
    peer_ids = jnp.arange(node_count, dtype=jnp.int32)
    member = (owners[None, :] == peer_ids[:, None]) & (peer_ids[:, None] != own_index)
    member_rank = jnp.cumsum(member.astype(jnp.int32), axis=1)
    slot_pos = jnp.arange(CAP, dtype=jnp.int32)
    matched = member[:, None, :] & (member_rank[:, None, :] == slot_pos[None, :, None] + 1)
    slot_index = jnp.arange(slot_count, dtype=jnp.int32)
    found_slot = jnp.sum(jnp.where(matched, slot_index[None, None, :], 0), axis=2)
    slot_live = jnp.any(matched, axis=2)
    peer_slots = jnp.where(slot_live, found_slot, -1)
    safe_slots = jnp.where(slot_live, peer_slots, 0)
    asked_blocks = jnp.where(slot_live, local_block[safe_slots], 0)
    every_block = lax.all_gather(proj, "nodes", axis=0, tiled=True)
    sources = every_block.reshape(-1, block_size, col_width)[tile_col]
    partials = jnp.einsum("sij,sjf->sif", adj_tiles, sources, preferred_element_type=jnp.float32)
    row_onehot = (tile_row[:, None] == block_ids[None, :]).astype(jnp.float32)
    pre_act = jnp.einsum("sr,sif->rif", row_onehot, partials, precision=highest).reshape(
        node_rows, col_width
    )
    activated = jax.nn.silu(pre_act).astype(jnp.bfloat16)
    sigmoid_vals = jax.nn.sigmoid(pre_act)
    grad_pre = (
        cotangent.astype(jnp.float32) * sigmoid_vals * (1.0 + pre_act * (1.0 - sigmoid_vals))
    ).astype(jnp.bfloat16)
    grad_blocks = grad_pre.reshape(blocks_here, block_size, col_width)
    back_terms = jnp.einsum(
        "sji,sjf->sif", adj_tiles, grad_blocks[tile_row], preferred_element_type=jnp.float32
    )
    local_onehot = (
        (owners == own_index)[:, None] & (local_block[:, None] == block_ids[None, :])
    ).astype(jnp.float32)
    grad_total = jnp.einsum("sc,sif->cif", local_onehot, back_terms, precision=highest)
    send_terms = back_terms[safe_slots] * slot_live[:, :, None, None].astype(jnp.float32)
    received, received_ids = (
        lax.all_to_all(send_terms, "nodes", split_axis=0, concat_axis=0, tiled=True),
        lax.all_to_all(asked_blocks, "nodes", split_axis=0, concat_axis=0, tiled=True),
    )
    recv_onehot = (received_ids.reshape(-1)[:, None] == block_ids[None, :]).astype(jnp.float32)
    grad_total = grad_total + jnp.einsum(
        "mc,mif->cif", recv_onehot, received.reshape(-1, block_size, col_width), precision=highest
    )
    grad_proj = grad_total.reshape(node_rows, col_width).astype(jnp.bfloat16)
    weight_term = jnp.einsum("nk,nf->kf", full_rows, grad_proj, preferred_element_type=jnp.float32)
    grad_weight = lax.psum(weight_term, "nodes") / math.sqrt(node_rows * node_count)
    input_terms = jnp.einsum("nf,kf->nk", grad_proj, weight, preferred_element_type=jnp.float32)
    grad_features = lax.psum_scatter(input_terms, "feat", scatter_dimension=1, tiled=True).astype(
        jnp.bfloat16
    )
    return (activated, grad_features, grad_weight)


def solution(mesh):
    return jax.shard_map(
        per_device,
        mesh=mesh,
        in_specs=(
            P("nodes", "feat"),
            P(None, "feat"),
            P("nodes", None, None),
            P("nodes"),
            P("nodes"),
            P("nodes", "feat"),
        ),
        out_specs=(P("nodes", "feat"), P("nodes", "feat"), P(None, "feat")),
        check_vma=False,
    )
```

profile of v0, /device:TPU:1, one launch (start us, length us, event | category | flops | bytes accessed | tf_op | source)
XLA Modules:
  0.0 515.8 jit_solution(13034335589992170231)
XLA Ops:
  7.2 0.0 all-gather.3.cloned.1.call-start
  7.2 0.7 all-gather.3.cloned.1.call-update
  7.9 0.0 all-gather.5.cloned.1.call-start
  8.0 53.0 %all-gather.3.cloned.1.call-done = bf16[8192,256]{0,1:T(8,128)(2,1)} async-done(((bf16[8192,64]{0,1:T(8,128)(2,1)}), bf16[8192,256]{0,1:T(8,128)(2,1)}) %all-gather.3.cloned.1.call-update) | async-done | bytes 4194320 | tf_op jit(solution)/shard_map/all_gather | solution.py:21
  60.9 4.0 convolution_convert_fusion
  65.0 0.0 all-gather.5.cloned.1.call-update
  65.0 0.1 fusion.27
  65.1 0.9 reduce-window.6
  66.0 0.2 slice_reduce_fusion
  66.2 0.1 fusion.25
  66.3 0.1 copy_bitcast_fusion.2
  66.4 0.2 fusion.22
  66.6 0.2 select_reduce_fusion
  66.8 0.1 copy.48
  66.9 0.1 reshape.159
  67.0 0.8 gather_fusion.2
  67.8 0.1 reshape.158
  67.9 0.1 copy.49
  68.0 0.7 copy.50
  68.7 7.8 %all-to-all-start = ((s32[32,1,2]{2,1,0:T(1,128)}), s32[32,1,2]{2,1,0:T(1,128)S(1)}, u32[]{:S(2)}, u32[]{:S(2)}) async-start(s32[32,1,2]{2,1,0:T(1,128)} %copy.50), calls=%async_computation | async-start | bytes 32768 | tf_op jit(solution)/shard_map/all_to_all | solution.py:59
  76.6 0.1 copy.51
  76.7 103.2 %all-gather.5.cloned.1.call-done = bf16[262144,64]{0,1:T(8,128)(2,1)} async-done(((bf16[8192,64]{0,1:T(8,128)(2,1)}), bf16[262144,64]{0,1:T(8,128)(2,1)}) %all-gather.5.cloned.1.call-update) | async-done | bytes 33554448 | tf_op jit(solution)/shard_map/all_gather | solution.py:36
  179.9 23.1 %copy_bitcast_fusion = bf16[2048,128,64]{1,2,0:T(8,128)(2,1)} fusion(bf16[262144,64]{0,1:T(8,128)(2,1)} %all-gather.5.cloned.1.call-done), kind=kLoop, calls=%fused_computation.4 | loop fusion | bytes 67108864 | tf_op jit(solution)/shard_map/reshape | solution.py:37
  202.9 16.8 %gather_fusion = bf16[384,128,64]{1,2,0:T(8,128)(2,1)} fusion(bf16[2048,128,64]{1,2,0:T(8,128)(2,1)} %copy_bitcast_fusion, s32[1024]{0:T(1024)S(1)} %pad_clamp_fusion.2), kind=kCustom, calls=%fused_computation | custom fusion | bytes 12584448 | tf_op jit(solution)/shard_map/gather | solution.py:37
  219.7 15.3 %convolution_bitcast_fusion.1 = f32[384,128,64]{1,2,0:T(8,128)} fusion(bf16[384,128,64]{1,2,0:T(8,128)(2,1)} %gather_fusion, bf16[384,128,128]{2,1,0:T(8,128)(2,1)} %param.8), kind=kOutput, calls=%fused_computation.11 | convolution fusion | flops 805306368 | bytes 31457280 | tf_op jit(solution)/shard_map/sij,sjf->sif/dot_general | solution.py:38
  235.0 16.6 %fusion.2 = f32[64,128,64]{1,0,2:T(8,128)S(1)} fusion(f32[384,128,64]{1,2,0:T(8,128)} %convolution_bitcast_fusion.1, s32[384]{0:T(512)S(1)} %copy-done.4), kind=kOutput, calls=%fused_computation.7 | convolution fusion | flops 2415943680 | bytes 14681600 | tf_op jit(solution)/shard_map/sr,sif->rif/dot_general | solution.py:40
  251.5 2.8 fusion.14
  254.4 0.3 copy.77
  254.7 13.5 %gather_fusion.1 = bf16[384,128,64]{1,2,0:T(8,128)(2,1)} fusion(bf16[64,128,64]{1,2,0:T(8,128)(2,1)S(1)} %bitcast.91, s32[1024]{0:T(1024)S(1)} %pad_clamp_fusion.1), kind=kCustom, calls=%fused_computation.1 | custom fusion | bytes 12584448 | tf_op jit(solution)/shard_map/gather | solution.py:50
  268.2 14.4 %convolution_bitcast_fusion = f32[384,128,64]{1,2,0:T(8,128)} fusion(bf16[384,128,64]{1,2,0:T(8,128)(2,1)} %gather_fusion.1, bf16[384,128,128]{2,1,0:T(8,128)(2,1)} %param.8), kind=kOutput, calls=%fused_computation.10 | convolution fusion | flops 805306368 | bytes 31457280 | tf_op jit(solution)/shard_map/sji,sjf->sif/dot_general | solution.py:49
  282.6 5.3 %gather_fusion.3 = f32[64,128,64]{1,2,0:T(8,128)S(1)} fusion(f32[384,128,64]{1,2,0:T(8,128)} %convolution_bitcast_fusion, s32[1024]{0:T(1024)S(1)} %pad_clamp_fusion), kind=kCustom, calls=%fused_computation.3 | custom fusion | bytes 4194560 | tf_op jit(solution)/shard_map/gather | solution.py:56
  287.8 1.5 broadcast_multiply_fusion
  289.4 5.6 %all-to-all-start.1 = ((f32[32,2,128,64]{2,3,1,0:T(8,128)}), f32[32,2,128,64]{2,3,1,0:T(8,128)}, u32[]{:S(2)}, u32[]{:S(2)}) async-start(f32[32,2,128,64]{2,3,1,0:T(8,128)} %broadcast_multiply_fusion), calls=%async_computation.1 | async-start | bytes 4194304 | tf_op jit(solution)/shard_map/all_to_all | solution.py:58
  294.9 0.0 all-reduce.2.cloned.1.call-start
  295.0 0.5 broadcast.133
  295.5 0.7 reduce.5
  296.2 0.1 eq.104
  296.3 16.3 %fusion = f32[64,128,64]{1,0,2:T(8,128)S(1)} fusion(f32[384,128,64]{1,2,0:T(8,128)} %convolution_bitcast_fusion, s32[384]{0:T(512)S(1)} %get-tuple-element.7, pred[384]{0:T(512)(128)(4,1)S(1)} %get-tuple-element.3), kind=kOutput, calls=%fused_computation.5 | convolution fusion | flops 2415968256 | bytes 14681984 | tf_op jit(solution)/shard_map/sc,sif->cif/dot_general | solution.py:55
  312.6 10.8 %all-to-all-done.1 = f32[32,2,128,64]{2,3,1,0:T(8,128)} async-done(((f32[32,2,128,64]{2,3,1,0:T(8,128)}), f32[32,2,128,64]{2,3,1,0:T(8,128)}, u32[]{:S(2)}, u32[]{:S(2)}) %all-to-all-start.1) | async-done | bytes 2097184 | tf_op jit(solution)/shard_map/all_to_all | solution.py:58
  323.3 3.4 copy.52
  326.7 1.4 add_convert_fusion
  328.2 2.0 convolution_bitcast_fusion.2
  330.2 0.0 reduce-scatter.2.cloned.1.call-start
  330.3 4.5 fusion.12
  334.8 90.1 %all-reduce.2.cloned.1.call-done = f32[256,64]{0,1:T(8,128)} async-done(((f32[256,64]{0,1:T(8,128)}), f32[256,64]{0,1:T(8,128)}) %all-reduce.2.cloned.1.call-update) | async-done | bytes 65552 | tf_op jit(solution)/shard_map/psum | solution.py:67
  424.9 1.5 broadcast_multiply_fusion.1
  426.4 79.9 %reduce-scatter.2.cloned.1.call-done = f32[8192,64]{0,1:T(8,128)} async-done(((f32[8192,256]{0,1:T(8,128)}), f32[8192,64]{0,1:T(8,128)}) %reduce-scatter.2.cloned.1.call-update) | async-done | bytes 2097168 | tf_op jit(solution)/shard_map/reduce_scatter | solution.py:69
  506.4 2.7 convert_element_type.44
  (25 shorter events, 0.2 us)
Async XLA Ops:
  7.2 53.8 %copy-start = (bf16[256,64]{0,1:T(8,128)(2,1)S(1)}, bf16[256,64]{0,1:T(8,128)(2,1)}, u32[]{:S(2)}) copy-start(bf16[256,64]{0,1:T(8,128)(2,1)} %param.7) | copy-start | bytes 98308
  7.2 57.8 %copy-start.3 = (s32[384]{0:T(512)S(1)}, s32[384]{0:T(512)}, u32[]{:S(2)}) copy-start(s32[384]{0:T(512)} %param.10) | copy-start | bytes 4612
  7.2 53.8 %all-gather.3.cloned.1.call-start = ((), (), s32[]{:S(2)}) async-start(), calls=%async_computation.3 | async-start | bytes 5242880 | tf_op jit(solution)/shard_map/all_gather | solution.py:21
  7.9 171.9 %all-gather.5.cloned.1.call-start = ((), (), s32[]{:S(2)}) async-start(), calls=%async_computation.4 | async-start | bytes 34603008 | tf_op jit(solution)/shard_map/all_gather | solution.py:36
  67.0 9.7 %copy-start.4 = (s32[384]{0:T(512)S(1)}, s32[384]{0:T(512)}, u32[]{:S(2)}) copy-start(s32[384]{0:T(512)} %param.9) | copy-start | bytes 4612
  68.7 220.7 %all-to-all-start = ((s32[32,1,2]{2,1,0:T(1,128)}), s32[32,1,2]{2,1,0:T(1,128)S(1)}, u32[]{:S(2)}, u32[]{:S(2)}) async-start(s32[32,1,2]{2,1,0:T(1,128)} %copy.50), calls=%async_computation | async-start | bytes 32768 | tf_op jit(solution)/shard_map/all_to_all | solution.py:59
  235.0 16.6 %copy-start.2 = (bf16[8192,64]{0,1:T(8,128)(2,1)S(1)}, bf16[8192,64]{0,1:T(8,128)(2,1)}, u32[]{:S(2)}) copy-start(bf16[8192,64]{0,1:T(8,128)(2,1)} %param.11) | copy-start | bytes 3145732
  289.4 34.0 %all-to-all-start.1 = ((f32[32,2,128,64]{2,3,1,0:T(8,128)}), f32[32,2,128,64]{2,3,1,0:T(8,128)}, u32[]{:S(2)}, u32[]{:S(2)}) async-start(f32[32,2,128,64]{2,3,1,0:T(8,128)} %broadcast_multiply_fusion), calls=%async_computation.1 | async-start | bytes 4194304 | tf_op jit(solution)/shard_map/all_to_all | solution.py:58
  294.9 130.0 %all-reduce.2.cloned.1.call-start = ((), (), s32[]{:S(2)}) async-start(), calls=%async_computation.6 | async-start | bytes 131072 | tf_op jit(solution)/shard_map/psum | solution.py:67
  323.3 4.8 copy-start.1
  330.2 176.2 %reduce-scatter.2.cloned.1.call-start = ((), (), s32[]{:S(2)}) async-start(), calls=%async_computation.5 | async-start | bytes 10485760 | tf_op jit(solution)/shard_map/reduce_scatter | solution.py:69
Sparse Core Ops, SparseCore 0:
  9.7 51.2 all-gather.2
  65.1 114.7 all-gather.4
  330.3 94.5 all-reduce.1
  427.3 79.0 reduce-scatter.1
where the time goes:
time: 523 us; the launch traced here: 516 us
  waiting for transfers between devices  338 us (65%)
  matrix products  74.5 us (14%)
  local copies, waits for them, and re-layouts  65.1 us (12%)
  between operations  14.2 us (3%)
  starting transfers between devices  13.5 us (3%)
  other arithmetic  10.8 us (2%)
    all_gather x1, waiting for transfers between devices, per_device(): every_block = lax.all_gather(proj, 'nodes', axis=0, tiled=True)  103 us
    psum x1, waiting for transfers between devices, per_device(): lax.psum(weight_term, 'nodes') / math.sqrt(node_rows * node_count)  90.1 us
    reduce_scatter x1, waiting for transfers between devices, per_device(): lax.psum_scatter(input_terms, 'feat', scatter_dimension=1, tiled=True)  79.9 us
    all_gather x1, waiting for transfers between devices, per_device(): full_rows = lax.all_gather(features, 'feat', axis=1, tiled=True)  53 us
    reshape x1, local copies, waits for them, and re-layouts, per_device(): sources = every_block.reshape(-1, block_size, col_width)[tile_col]  23.1 us
    gather x1, local copies, waits for them, and re-layouts, per_device(): sources = every_block.reshape(-1, block_size, col_width)[tile_col]  16.8 us
    dot_general x1, matrix products, per_device(): jnp.einsum('sr,sif->rif', row_onehot, partials, precision=highest)  16.6 us
    dot_general x1, matrix products, per_device(): jnp.einsum('sc,sif->cif', local_onehot, back_terms, precision=highest)  16.3 us
  transfers between devices with their start and end apart: 6, of which 5 were waited for; matrix products, arithmetic and copies ran while one was open for 27% of the time, Pallas kernels for 0%

commit v1 on v0

v1 whole, which is shorter than its diff:
```python
import functools
import math

import jax
import jax.numpy as jnp
from jax import lax
from jax.experimental import pallas as pl
from jax.experimental.pallas import tpu as pltpu
from jax.sharding import PartitionSpec as P

CAP = 2
STEP = 32
VMEM = pltpu.MemorySpace.VMEM
NT = (((1,), (1,)), ((), ()))
NN = (((1,), (0,)), ((), ()))


def whole():
    return pl.BlockSpec(memory_space=VMEM)


def params():
    return pltpu.CompilerParams(vmem_limit_bytes=48 * 1024 * 1024)


def proj_kernel(ids, wt_ref, x_ref, proj_ref, send_ref):
    step = pl.program_id(0)
    made = jnp.dot(wt_ref[...], x_ref[...], preferred_element_type=jnp.float32)
    made = made.astype(jnp.bfloat16)
    per_step = x_ref.shape[1] // 128
    for b in range(per_step):
        proj_ref[step * per_step + b] = made[:, b * 128 : (b + 1) * 128]

    @pl.when(step == pl.num_programs(0) - 1)
    def _():
        @pl.loop(0, send_ref.shape[0], unroll=4)
        def _(e):
            send_ref[e] = proj_ref[ids[e]]


def project(ids, wt, full_t, blocks):
    width, depth = wt.shape
    nodes = full_t.shape[1]
    chunk = 1024
    entries = ids.shape[0]
    return pl.pallas_call(
        proj_kernel,
        grid_spec=pltpu.PrefetchScalarGridSpec(
            num_scalar_prefetch=1,
            grid=(nodes // chunk,),
            in_specs=[
                pl.BlockSpec((width, depth), lambda i, ids: (0, 0)),
                pl.BlockSpec((depth, chunk), lambda i, ids: (0, i)),
            ],
            out_specs=[
                pl.BlockSpec((blocks, width, 128), lambda i, ids: (0, 0, 0)),
                pl.BlockSpec((entries, width, 128), lambda i, ids: (0, 0, 0)),
            ],
        ),
        out_shape=[
            jax.ShapeDtypeStruct((blocks, width, 128), jnp.bfloat16),
            jax.ShapeDtypeStruct((entries, width, 128), jnp.bfloat16),
        ],
        compiler_params=params(),
        cost_estimate=pl.CostEstimate(
            flops=2 * nodes * depth * width, bytes_accessed=12 << 20, transcendentals=0
        ),
        name="project",
    )(ids, wt, full_t)


def tile_kernel(dims, src, dst, x_ref, tile_ref, acc_ref, part_ref):
    step = pl.program_id(0)

    @pl.when(step == 0)
    def _():
        acc_ref[...] = jnp.zeros_like(acc_ref)

    base = step * STEP
    for t in range(STEP):
        part_ref[t] = lax.dot_general(
            x_ref[src[base + t]], tile_ref[t], dims, preferred_element_type=jnp.float32
        )
    for t in range(STEP):
        acc_ref[dst[base + t]] += part_ref[t]


def local_tiles(dims, src, dst, x, tiles, name):
    blocks, width, size = x.shape
    count = tiles.shape[0]
    return pl.pallas_call(
        functools.partial(tile_kernel, dims),
        grid_spec=pltpu.PrefetchScalarGridSpec(
            num_scalar_prefetch=2,
            grid=(count // STEP,),
            in_specs=[
                pl.BlockSpec((blocks, width, size), lambda i, s, d: (0, 0, 0)),
                pl.BlockSpec((STEP, size, size), lambda i, s, d: (i, 0, 0)),
            ],
            out_specs=pl.BlockSpec((blocks + 1, width, size), lambda i, s, d: (0, 0, 0)),
            scratch_shapes=[pltpu.VMEM((STEP, width, size), jnp.float32)],
        ),
        out_shape=jax.ShapeDtypeStruct((blocks + 1, width, size), jnp.float32),
        compiler_params=params(),
        cost_estimate=pl.CostEstimate(
            flops=8 * count * size * size * width, bytes_accessed=20 << 20, transcendentals=0
        ),
        name=name,
    )(src, dst, x, tiles)


def middle_kernel(
    slots, rows, acc_ref, recv_ref, cot_ref, tiles_ref, act_ref, grad_ref, send_ref,
    held, extra, grads, part, sems,
):
    entries = recv_ref.shape[0]
    blocks = grad_ref.shape[0]

    @pl.loop(0, entries)
    def _(e):
        pltpu.make_async_copy(tiles_ref.at[slots[e]], held.at[e], sems.at[e]).start()

    extra[...] = jnp.zeros_like(extra)
    grads[blocks] = jnp.zeros_like(grads[blocks])

    @pl.loop(0, entries)
    def _(e):
        pltpu.make_async_copy(tiles_ref.at[slots[e]], held.at[e], sems.at[e]).wait()

    @pl.loop(0, entries // 16)
    def _(g):
        for t in range(16):
            part[t] = lax.dot_general(
                recv_ref[g * 16 + t], held[g * 16 + t], NT, preferred_element_type=jnp.float32
            )
        for t in range(16):
            extra[rows[g * 16 + t]] += part[t]

    @pl.loop(0, blocks, unroll=2)
    def _(b):
        cols = pl.ds(pl.multiple_of(b * 128, 128), 128)
        v = acc_ref[b] + extra[b]
        s = jax.nn.sigmoid(v)
        act_ref[:, cols] = (v * s).astype(jnp.bfloat16)
        grad = cot_ref[:, cols].astype(jnp.float32) * s * (1.0 + v * (1.0 - s))
        grad = grad.astype(jnp.bfloat16)
        grads[b] = grad
        grad_ref[b] = grad

    @pl.loop(0, entries // 16)
    def _(g):
        for t in range(16):
            send_ref[g * 16 + t] = lax.dot_general(
                grads[rows[g * 16 + t]], held[g * 16 + t], NN,
                preferred_element_type=jnp.float32,
            ).astype(jnp.bfloat16)


def middle(slots, rows, acc, recv, cot_t, tiles):
    entries, width, size = recv.shape
    blocks = acc.shape[0] - 1
    nodes = cot_t.shape[1]
    return pl.pallas_call(
        middle_kernel,
        grid_spec=pltpu.PrefetchScalarGridSpec(
            num_scalar_prefetch=2,
            grid=(),
            in_specs=[whole(), whole(), whole(), pl.BlockSpec(memory_space=pl.ANY)],
            out_specs=[whole(), whole(), whole()],
            scratch_shapes=[
                pltpu.VMEM((entries, size, size), jnp.bfloat16),
                pltpu.VMEM((blocks + 1, width, size), jnp.float32),
                pltpu.VMEM((blocks + 1, width, size), jnp.bfloat16),
                pltpu.VMEM((16, width, size), jnp.float32),
                pltpu.SemaphoreType.DMA((entries,)),
            ],
        ),
        out_shape=[
            jax.ShapeDtypeStruct((width, nodes), jnp.bfloat16),
            jax.ShapeDtypeStruct((blocks, width, size), jnp.bfloat16),
            jax.ShapeDtypeStruct((entries, width, size), jnp.bfloat16),
        ],
        compiler_params=params(),
        name="middle",
    )(slots, rows, acc, recv, cot_t, tiles)


def finish_kernel(ids, acc_ref, recv_ref, out_ref, extra):
    extra[...] = jnp.zeros_like(extra)

    @pl.loop(0, recv_ref.shape[0], unroll=4)
    def _(e):
        extra[ids[e]] += recv_ref[e].astype(jnp.float32)

    @pl.loop(0, extra.shape[0], unroll=4)
    def _(b):
        cols = pl.ds(pl.multiple_of(b * 128, 128), 128)
        out_ref[:, cols] = (acc_ref[b] + extra[b]).astype(jnp.bfloat16)


def finish(ids, acc, recv):
    entries, width, size = recv.shape
    blocks = acc.shape[0] - 1
    return pl.pallas_call(
        finish_kernel,
        grid_spec=pltpu.PrefetchScalarGridSpec(
            num_scalar_prefetch=1,
            grid=(),
            in_specs=[whole(), whole()],
            out_specs=whole(),
            scratch_shapes=[pltpu.VMEM((blocks, width, size), jnp.float32)],
        ),
        out_shape=jax.ShapeDtypeStruct((width, blocks * size), jnp.bfloat16),
        compiler_params=params(),
        name="finish",
    )(ids, acc, recv)


def per_device(features, weight, adj_tiles, tile_row, tile_col, cotangent):
    block_size = adj_tiles.shape[1]
    node_rows = features.shape[0]
    blocks = node_rows // block_size
    width = features.shape[1]
    slot_count = adj_tiles.shape[0]
    node_count = lax.axis_size("nodes")
    own = lax.axis_index("nodes")
    feat_index = lax.axis_index("feat")

    owners = tile_col // blocks
    local_block = tile_col - owners * blocks
    slot_ids = jnp.arange(slot_count, dtype=jnp.int32)
    peers = jnp.arange(node_count, dtype=jnp.int32)
    member = (owners[None, :] == peers[:, None]) & (peers[:, None] != own)
    first = jnp.min(jnp.where(member, slot_ids[None, :], slot_count), axis=1)
    last = jnp.max(jnp.where(member, slot_ids[None, :], -1), axis=1)
    found = jnp.stack([first, last], axis=1)
    live = jnp.stack([last >= 0, last > first], axis=1)
    slots = jnp.where(live, found, 0).reshape(-1)
    live = live.reshape(-1)
    hit = slots[:, None] == slot_ids[None, :]
    slot_rows = jnp.sum(jnp.where(hit, tile_row[None, :], 0), axis=1)
    slot_blocks = jnp.sum(jnp.where(hit, local_block[None, :], 0), axis=1)
    rows = jnp.where(live, slot_rows, blocks).astype(jnp.int32)
    asked = jnp.where(live, slot_blocks, 0).astype(jnp.int32)
    every_asked = lax.all_gather(asked, "nodes", axis=0, tiled=False)
    ids = lax.dynamic_slice_in_dim(every_asked, own * CAP, CAP, 1).reshape(-1)

    is_local = owners == own
    src_fwd = jnp.where(is_local, local_block, 0)
    dst_fwd = jnp.where(is_local, tile_row, blocks)
    dst_bwd = jnp.where(is_local, local_block, blocks)

    wt = weight.T
    full_t = lax.all_gather(features.T, "feat", axis=0, tiled=True)
    full_wt = lax.all_gather(wt, "feat", axis=0, tiled=True)
    weight_part = lax.dynamic_slice_in_dim(full_wt, feat_index * width, width, 1)

    proj, send = project(ids, wt, full_t, blocks)
    recv = lax.all_to_all(send, "nodes", split_axis=0, concat_axis=0, tiled=True)
    acc = local_tiles(NT, src_fwd, dst_fwd, proj, adj_tiles, "forward_local")
    act_t, grads, send_back = middle(slots, rows, acc, recv, cotangent.T, adj_tiles)
    recv_back = lax.all_to_all(send_back, "nodes", split_axis=0, concat_axis=0, tiled=True)
    back = local_tiles(NN, tile_row, dst_bwd, grads, adj_tiles, "backward_local")
    gp_t = finish(ids, back, recv_back)
    gp_full = lax.all_gather(gp_t, "feat", axis=0, tiled=True)
    term = jnp.einsum("fn,kn->fk", gp_t, full_t, preferred_element_type=jnp.float32)
    grad_weight = lax.psum(term, "nodes") / math.sqrt(node_rows * node_count)
    gf_t = jnp.einsum("fk,fn->kn", weight_part, gp_full, preferred_element_type=jnp.float32)
    return (act_t.T, gf_t.astype(jnp.bfloat16).T, grad_weight.T)


def solution(mesh):
    return jax.shard_map(
        per_device,
        mesh=mesh,
        in_specs=(
            P("nodes", "feat"),
            P(None, "feat"),
            P("nodes", None, None),
            P("nodes"),
            P("nodes"),
            P("nodes", "feat"),
        ),
        out_specs=(P("nodes", "feat"), P("nodes", "feat"), P(None, "feat")),
        check_vma=False,
    )
```

time: 523 us -> 290 us (0.55); the launches traced: 516 us -> 288 us
  waiting for transfers between devices: 338 us -> 165 us
  matrix products: 74.5 us -> 8.67 us
  local copies, waits for them, and re-layouts: 65.1 us -> 5.98 us
  Pallas kernels: 0 us -> 44.6 us
  blocking collectives: 0 us -> 33.3 us
  other arithmetic: 10.8 us -> 3.29 us
    all_gather x2, waiting for transfers between devices: 156 us -> 73.7 us  [the longest x1 47.5 us: per_device(): gp_full = lax.all_gather(gp_t, 'feat', axis=0, tiled=True)]
    reduce_scatter x1 -> x0, waiting for transfers between devices: 79.9 us -> none  [per_device(): lax.psum_scatter(input_terms, 'feat', scatter_dimension=1, tiled=True)]
    dot_general x8 -> x2, matrix products: 74.5 us -> 8.67 us  [the longest x1 4.54 us: per_device(): jnp.einsum('fn,kn->fk', gp_t, full_t, preferred_element_type=jnp.float32)]
    pallas_call x0 -> x5, Pallas kernels: none -> 44.6 us  [the longest x2 25.7 us: local_tiles(): pl.pallas_call(functools.partial(tile_kernel, dims), grid_spec=pltpu.Pref...]
    gather x6 -> x0, local copies, waits for them, and re-layouts: 36.5 us -> none  [the longest x1 16.8 us: per_device(): sources = every_block.reshape(-1, block_size, col_width)[tile_col]]
    all_gather x0 -> x2, blocking collectives: none -> 33.3 us  [the longest x1 24.2 us: per_device(): every_asked = lax.all_gather(asked, 'nodes', axis=0, tiled=False)]
    reshape x2, local copies, waits for them, and re-layouts: 23.3 us -> 0.22 us  [the longest x1 0.11 us: per_device(): live = live.reshape(-1)]
    psum x1, waiting for transfers between devices: 90.1 us -> 84 us  [per_device(): grad_weight = lax.psum(term, 'nodes') / math.sqrt(node_rows * node_count)]
  transfers between devices with their start and end apart: 6 -> 5, of which waited for: 5 -> 5; matrix products, arithmetic and copies ran while one was open for 27% -> 1% of each run, Pallas kernels for 0% -> 9%
where the time goes in v1:
time: 290 us; the launch traced here: 288 us
  waiting for transfers between devices  165 us (57%)
  Pallas kernels  44.6 us (15%)
  blocking collectives  33.3 us (11%)
  starting transfers between devices  14.1 us (5%)
  between operations  13.9 us (5%)
  matrix products  8.67 us (3%)
  local copies, waits for them, and re-layouts  5.98 us (2%)
  other arithmetic  3.29 us (1%)
    psum x1, waiting for transfers between devices, per_device(): grad_weight = lax.psum(term, 'nodes') / math.sqrt(node_rows * node_count)  84 us
    all_gather x1, waiting for transfers between devices, per_device(): gp_full = lax.all_gather(gp_t, 'feat', axis=0, tiled=True)  47.5 us
    all_gather x1, waiting for transfers between devices, per_device(): full_t = lax.all_gather(features.T, 'feat', axis=0, tiled=True)  26.2 us
    pallas_call x2, Pallas kernels, local_tiles(): pl.pallas_call(functools.partial(tile_kernel, dims), grid_spec=pltpu.Pref...  25.7 us
    all_gather x1, blocking collectives, per_device(): every_asked = lax.all_gather(asked, 'nodes', axis=0, tiled=False)  24.2 us
    pallas_call x1, Pallas kernels, middle(): pl.pallas_call(middle_kernel, grid_spec=pltpu.PrefetchScalarGridSpec(num_...  9.55 us
    all_gather x1, blocking collectives, per_device(): full_wt = lax.all_gather(wt, 'feat', axis=0, tiled=True)  9.11 us
    all_to_all x1, starting transfers between devices, per_device(): lax.all_to_all(send, 'nodes', split_axis=0, concat_axis=0, tiled=True)  7.83 us
  transfers between devices with their start and end apart: 5, of which 5 were waited for; matrix products, arithmetic and copies ran while one was open for 1% of the time, Pallas kernels for 9%

profile of v1, /device:TPU:1, one launch (start us, length us, event | category | flops | bytes accessed | tf_op | source)
XLA Modules:
  0.0 288.4 jit_solution(8906121670567845552)
XLA Ops:
  7.2 0.0 copy-start.7
  7.2 0.0 all-gather.4.cloned.1.call-start
  7.2 0.7 all-gather.4.cloned.1.call-update
  7.9 0.7 broadcast_select_fusion
  8.6 0.2 select_reduce_fusion.3
  8.9 0.1 copy.18
  9.0 0.1 stack.15
  9.1 0.1 reshape.64
  9.2 0.1 copy.19
  9.3 0.1 stack.17
  9.4 0.9 select_reduce_fusion
  10.3 24.2 %all-gather = s32[32,1,64]{2,1,0:T(1,128)S(1)} all-gather(s32[1,1,64]{2,1,0:T(1,128)S(1)} %fusion.4), channel_id=1, replica_groups=mesh['nodes'=32,'feat'=4] {'nodes'}, dimensions={0}, use_global_device_ids=true | all-gather | bytes 8448 | tf_op jit(solution)/shard_map/all_gather | solution.py:245
  34.5 0.1 dynamic-slice_reduce_fusion
  34.6 0.1 reshape.65.ids
  34.7 26.2 %all-gather.4.cloned.1.call-done.x_ref = bf16[256,8192]{1,0:T(8,128)(2,1)} async-done(((bf16[64,8192]{1,0:T(8,128)(2,1)}), bf16[256,8192]{1,0:T(8,128)(2,1)}) %all-gather.4.cloned.1.call-update) | async-done | bytes 4194320 | tf_op jit(solution)/shard_map/all_gather | solution.py:254
  60.9 0.0 copy-start.5
  60.9 0.8 copy-done.5
  61.7 7.0 %project.1 = (bf16[64,64,128]{2,1,0:T(8,128)(2,1)S(1)}, bf16[64,64,128]{2,1,0:T(8,128)(2,1)}) custom-call(s32[64]{0:T(128)S(1)} %reshape.65.ids, bf16[64,256]{1,0:T(8,128)(2,1)S(1)} %bitcast.21, bf16[256,8192]{1,0:T(8,128)(2,1)} %all-gather.4.cloned.1.call-done.x_ref), custom_call_target="tpu_custom_call" | custom-call | flops 268435456 | bytes 12582912 | tf_op jit(solution)/shard_map/project/pallas_call | solution.py:46
  68.7 7.8 %all-to-all-start = ((bf16[64,64,128]{2,1,0:T(8,128)(2,1)}), bf16[64,64,128]{2,1,0:T(8,128)(2,1)S(1)}, u32[]{:S(2)}, u32[]{:S(2)}) async-start(bf16[64,64,128]{2,1,0:T(8,128)(2,1)} %get-tuple-element.9), calls=%async_computation | async-start | bytes 2097152 | tf_op jit(solution)/shard_map/all_to_all | solution.py:259
  76.6 0.0 copy-done.7
  76.6 0.0 copy-start.1
  76.6 14.2 %forward_local.1.acc_ref = f32[65,64,128]{2,1,0:T(8,128)S(1)} custom-call(s32[384]{0:T(512)S(1)} %get-tuple-element.22.src, s32[384]{0:T(512)S(1)} %get-tuple-element.21.dst, bf16[64,64,128]{2,1,0:T(8,128)(2,1)S(1)} %get-tuple-element.8.x_ref, bf16[384,128,128]{2,1,0:T(8,128)(2,1)} %tile_ref.3), custom_call_target="tpu_custom_call" | custom-call | flops 3221225472 | bytes 20971520 | tf_op jit(solution)/shard_map/forward_local/pallas_call | solution.py:91
  90.8 0.0 copy-start
  90.8 1.3 copy-done
  92.2 1.3 all-to-all-done.recv_ref
  93.5 0.0 copy-done.1
  93.5 9.5 %middle.1 = (bf16[64,8192]{1,0:T(8,128)(2,1)}, bf16[64,64,128]{2,1,0:T(8,128)(2,1)S(1)}, bf16[64,64,128]{2,1,0:T(8,128)(2,1)S(1)}) custom-call(s32[64]{0:T(128)S(1)} %broadcast_select_fusion.4.slots, s32[64]{0:T(128)S(1)} %broadcast_select_fusion.3.rows, f32[65,64,128]{2,1,0:T(8,128)} %copy-done, bf16[64,64,128]{2,1,0:T(8,128)(2,1)S(1)} %all-to-all-done.recv_ref, ...), custom_call_target="tpu_custom_call" | custom-call | tf_op jit(solution)/shard_map/middle/pallas_call | solution.py:163
  103.0 0.0 copy-start.2
  103.0 1.0 copy-done.2
  104.0 0.0 copy-start.4
  104.0 1.0 copy-done.4
  105.0 6.2 %all-to-all-start.1 = ((bf16[64,64,128]{2,1,0:T(8,128)(2,1)}), bf16[64,64,128]{2,1,0:T(8,128)(2,1)S(1)}, u32[]{:S(2)}, u32[]{:S(2)}) async-start(bf16[64,64,128]{2,1,0:T(8,128)(2,1)} %copy-done.4), calls=%async_computation.1 | async-start | bytes 2097152 | tf_op jit(solution)/shard_map/all_to_all | solution.py:262
  111.1 0.0 all-reduce.2.cloned.1.call-start
  111.2 0.0 copy-start.3
  111.2 1.2 copy-done.3
  112.4 11.5 %backward_local.1.acc_ref = f32[65,64,128]{2,1,0:T(8,128)S(1)} custom-call(s32[384]{0:T(512)S(1)} %copy-done.7, s32[384]{0:T(512)S(1)} %get-tuple-element.17.dst, bf16[64,64,128]{2,1,0:T(8,128)(2,1)S(1)} %copy-done.3, bf16[384,128,128]{2,1,0:T(8,128)(2,1)} %tile_ref.3), custom_call_target="tpu_custom_call" | custom-call | flops 3221225472 | bytes 20971520 | tf_op jit(solution)/shard_map/backward_local/pallas_call | solution.py:91
  123.9 4.1 %all-to-all-done.1.recv_ref = bf16[64,64,128]{2,1,0:T(8,128)(2,1)S(1)} async-done(((bf16[64,64,128]{2,1,0:T(8,128)(2,1)}), bf16[64,64,128]{2,1,0:T(8,128)(2,1)S(1)}, u32[]{:S(2)}, u32[]{:S(2)}) %all-to-all-start.1) | async-done | bytes 1048608 | tf_op jit(solution)/shard_map/all_to_all | solution.py:262
  128.0 2.3 finish.1
  130.4 4.5 %fusion.6 = f32[64,256]{1,0:T(8,128)} fusion(bf16[64,8192]{1,0:T(8,128)(2,1)} %finish.1, bf16[256,8192]{1,0:T(8,128)(2,1)} %all-gather.4.cloned.1.call-done.x_ref), kind=kOutput, calls=%fused_computation.33 | convolution fusion | flops 268435456 | bytes 5308416 | tf_op jit(solution)/shard_map/fn,kn->fk/dot_general | solution.py:266
  134.9 0.0 all-reduce.2.cloned.1.call-update
  134.9 0.0 all-gather.6.cloned.1.call-start
  135.0 0.7 all-gather.6.cloned.1.call-update
  135.7 0.0 copy-done.6
  135.7 9.1 %all_gather.16 = bf16[256,256]{1,0:T(8,128)(2,1)S(1)} all-gather(bf16[64,256]{1,0:T(8,128)(2,1)S(1)} %bitcast.22), channel_id=1, replica_groups=mesh['nodes'=32,'feat'=4] {'feat'}, dimensions={0}, use_global_device_ids=true | all-gather | bytes 163840 | tf_op jit(solution)/shard_map/all_gather | solution.py:255
  144.8 84.0 %all-reduce.2.cloned.1.call-done = f32[64,256]{1,0:T(8,128)} async-done(((f32[64,256]{1,0:T(8,128)}), f32[64,256]{1,0:T(8,128)}) %all-reduce.2.cloned.1.call-update) | async-done | bytes 65552 | tf_op jit(solution)/shard_map/psum | solution.py:267
  228.8 1.5 multiply_bitcast_fusion
  230.3 47.5 %all-gather.6.cloned.1.call-done = bf16[256,8192]{1,0:T(8,128)(2,1)} async-done(((bf16[64,8192]{1,0:T(8,128)(2,1)}), bf16[256,8192]{1,0:T(8,128)(2,1)}) %all-gather.6.cloned.1.call-update) | async-done | bytes 4194320 | tf_op jit(solution)/shard_map/all_gather | solution.py:265
  277.8 4.1 %convolution_convert_fusion = bf16[8192,64]{0,1:T(8,128)(2,1)} fusion(bf16[256,8192]{1,0:T(8,128)(2,1)} %all-gather.6.cloned.1.call-done, bf16[256,256]{1,0:T(8,128)(2,1)S(1)} %all_gather.16, s32[]{:T(128)S(6)} %select_n.70), kind=kOutput, calls=%fused_computation | convolution fusion | flops 268959744 | bytes 5308420 | tf_op jit(solution)/shard_map/fk,fn->kn/dot_general | solution.py:268
  (9 shorter events, 0.1 us)
Async XLA Ops:
  7.2 69.4 %copy-start.7 = (s32[384]{0:T(512)S(1)}, s32[384]{0:T(512)}, u32[]{:S(2)}) copy-start(s32[384]{0:T(512)} %src.1) | copy-start | bytes 4612
  7.2 53.8 %all-gather.4.cloned.1.call-start = ((), (), s32[]{:S(2)}) async-start(), calls=%async_computation.2 | async-start | bytes 5242880 | tf_op jit(solution)/shard_map/all_gather | solution.py:254
  60.9 0.8 copy-start.5
  68.7 24.7 %all-to-all-start = ((bf16[64,64,128]{2,1,0:T(8,128)(2,1)}), bf16[64,64,128]{2,1,0:T(8,128)(2,1)S(1)}, u32[]{:S(2)}, u32[]{:S(2)}) async-start(bf16[64,64,128]{2,1,0:T(8,128)(2,1)} %get-tuple-element.9), calls=%async_computation | async-start | bytes 2097152 | tf_op jit(solution)/shard_map/all_to_all | solution.py:259
  76.6 16.9 %copy-start.1 = (bf16[8192,64]{0,1:T(8,128)(2,1)S(1)}, bf16[8192,64]{0,1:T(8,128)(2,1)}, u32[]{:S(2)}) copy-start(bf16[8192,64]{0,1:T(8,128)(2,1)} %param.11) | copy-start | bytes 3145732
  90.8 1.3 copy-start
  103.0 1.0 copy-start.2
  104.0 1.0 copy-start.4
  105.0 23.1 %all-to-all-start.1 = ((bf16[64,64,128]{2,1,0:T(8,128)(2,1)}), bf16[64,64,128]{2,1,0:T(8,128)(2,1)S(1)}, u32[]{:S(2)}, u32[]{:S(2)}) async-start(bf16[64,64,128]{2,1,0:T(8,128)(2,1)} %copy-done.4), calls=%async_computation.1 | async-start | bytes 2097152 | tf_op jit(solution)/shard_map/all_to_all | solution.py:262
  111.1 117.7 %all-reduce.2.cloned.1.call-start = ((), (), s32[]{:S(2)}) async-start(), calls=%async_computation.4 | async-start | bytes 131072 | tf_op jit(solution)/shard_map/psum | solution.py:267
  111.2 1.2 copy-start.3
  130.4 5.3 %copy-start.6 = (bf16[256,64]{0,1:T(8,128)(2,1)S(1)}, bf16[256,64]{0,1:T(8,128)(2,1)}, u32[]{:S(2)}) copy-start(bf16[256,64]{0,1:T(8,128)(2,1)} %param.7) | copy-start | bytes 98308
  134.9 142.8 %all-gather.6.cloned.1.call-start = ((), (), s32[]{:S(2)}) async-start(), calls=%async_computation.3 | async-start | bytes 5242880 | tf_op jit(solution)/shard_map/all_gather | solution.py:265
Sparse Core Ops, SparseCore 0:
  9.6 51.2 all-gather.3
  135.0 93.7 all-reduce.1
  231.1 46.6 all-gather.5

commit v2 on v1

--- a/solution.py
+++ b/solution.py
@@ -255,6 +255,7 @@
     full_wt = lax.all_gather(wt, "feat", axis=0, tiled=True)
     weight_part = lax.dynamic_slice_in_dim(full_wt, feat_index * width, width, 1)
 
+    wt, weight_part = lax.optimization_barrier((wt, weight_part))
     proj, send = project(ids, wt, full_t, blocks)
     recv = lax.all_to_all(send, "nodes", split_axis=0, concat_axis=0, tiled=True)
     acc = local_tiles(NT, src_fwd, dst_fwd, proj, adj_tiles, "forward_local")
@@ -264,7 +265,10 @@
     gp_t = finish(ids, back, recv_back)
     gp_full = lax.all_gather(gp_t, "feat", axis=0, tiled=True)
     term = jnp.einsum("fn,kn->fk", gp_t, full_t, preferred_element_type=jnp.float32)
-    grad_weight = lax.psum(term, "nodes") / math.sqrt(node_rows * node_count)
+    pieces = term.reshape(node_count, -1, 128)
+    pieces = lax.all_to_all(pieces, "nodes", split_axis=0, concat_axis=0, tiled=True)
+    piece = jnp.sum(pieces, axis=0) / math.sqrt(node_rows * node_count)
+    grad_weight = lax.all_gather(piece, "nodes", axis=0, tiled=True).reshape(term.shape)
     gf_t = jnp.einsum("fk,fn->kn", weight_part, gp_full, preferred_element_type=jnp.float32)
     return (act_t.T, gf_t.astype(jnp.bfloat16).T, grad_weight.T)
 

time: 290 us -> 189 us (0.65)
  waiting for transfers between devices: 165 us -> 27.8 us
  blocking collectives: 33.3 us -> 69.8 us
    psum x1 -> x0, waiting for transfers between devices: 84 us -> none  [per_device(): grad_weight = lax.psum(term, 'nodes') / math.sqrt(node_rows * node_count)]
    all_gather x1, waiting for transfers between devices: 47.5 us -> 6.44 us  [per_device(): gp_full = lax.all_gather(gp_t, 'feat', axis=0, tiled=True)]
    all_gather x0 -> x1, blocking collectives: none -> 22.6 us  [per_device(): lax.all_gather(piece, 'nodes', axis=0, tiled=True).reshape(term.shape)]
    all_to_all x0 -> x1, blocking collectives: none -> 11.1 us  [per_device(): lax.all_to_all(pieces, 'nodes', split_axis=0, concat_axis=0, tiled=True)]
    all_gather x1, waiting for transfers between devices: 26.2 us -> 15.2 us  [per_device(): full_t = lax.all_gather(features.T, 'feat', axis=0, tiled=True)]
  transfers between devices with their start and end apart: 5 -> 4, of which waited for: 5 -> 4; matrix products, arithmetic and copies ran while one was open for 1% -> 4% of each run, Pallas kernels for 9% -> 14%
where the time goes in v2:
time: 189 us; the launch traced here: 187 us
  blocking collectives  69.8 us (37%)
  Pallas kernels  44.8 us (24%)
  waiting for transfers between devices  27.8 us (15%)
  between operations  14.2 us (8%)
  starting transfers between devices  13.9 us (7%)
  matrix products  7.96 us (4%)
  local copies, waits for them, and re-layouts  6.78 us (4%)
    pallas_call x2, Pallas kernels, local_tiles(): pl.pallas_call(functools.partial(tile_kernel, dims), grid_spec=pltpu.Pref...  25.7 us
    all_gather x1, blocking collectives, per_device(): every_asked = lax.all_gather(asked, 'nodes', axis=0, tiled=False)  24.2 us
    all_gather x1, blocking collectives, per_device(): lax.all_gather(piece, 'nodes', axis=0, tiled=True).reshape(term.shape)  22.6 us
    all_gather x1, waiting for transfers between devices, per_device(): full_t = lax.all_gather(features.T, 'feat', axis=0, tiled=True)  15.2 us
    all_gather x1, blocking collectives, per_device(): full_wt = lax.all_gather(wt, 'feat', axis=0, tiled=True)  11.9 us
    all_to_all x1, blocking collectives, per_device(): lax.all_to_all(pieces, 'nodes', split_axis=0, concat_axis=0, tiled=True)  11.1 us
    pallas_call x1, Pallas kernels, middle(): pl.pallas_call(middle_kernel, grid_spec=pltpu.PrefetchScalarGridSpec(num_...  9.75 us
    all_to_all x1, starting transfers between devices, per_device(): lax.all_to_all(send, 'nodes', split_axis=0, concat_axis=0, tiled=True)  7.83 us
  transfers between devices with their start and end apart: 4, of which 4 were waited for; matrix products, arithmetic and copies ran while one was open for 4% of the time, Pallas kernels for 14%

profile of v2, /device:TPU:1, one launch (start us, length us, event | category | flops | bytes accessed | tf_op | source)
XLA Modules:
  0.0 187.2 jit_solution(8149627251686708181)
XLA Ops:
  7.2 0.0 copy-start.6
  7.2 0.0 all-gather.5.cloned.1.call-start
  7.2 0.7 all-gather.5.cloned.1.call-update
  7.9 0.7 broadcast_select_fusion
  8.6 0.2 select_reduce_fusion.3
  8.9 0.1 copy.18
  9.0 0.1 stack.15
  9.1 0.1 reshape.70
  9.2 0.1 copy.19
  9.3 0.1 stack.17
  9.4 0.9 select_reduce_fusion
  10.3 24.2 %all-gather = s32[32,1,64]{2,1,0:T(1,128)S(1)} all-gather(s32[1,1,64]{2,1,0:T(1,128)S(1)} %fusion.3), channel_id=1, replica_groups=mesh['nodes'=32,'feat'=4] {'nodes'}, dimensions={0}, use_global_device_ids=true | all-gather | bytes 8448 | tf_op jit(solution)/shard_map/all_gather | solution.py:245
  34.5 0.1 dynamic-slice_reduce_fusion
  34.6 0.1 reshape.71.ids
  34.7 11.9 %all_gather.17 = bf16[256,256]{1,0:T(8,128)(2,1)S(1)} all-gather(bf16[64,256]{1,0:T(8,128)(2,1)} %bitcast.23), channel_id=1, replica_groups=mesh['nodes'=32,'feat'=4] {'feat'}, dimensions={0}, use_global_device_ids=true | all-gather | bytes 163840 | tf_op jit(solution)/shard_map/all_gather | solution.py:255
  46.6 0.1 constant_dynamic-slice_fusion
  46.7 15.2 %all-gather.5.cloned.1.call-done.x_ref = bf16[256,8192]{1,0:T(8,128)(2,1)} async-done(((bf16[64,8192]{1,0:T(8,128)(2,1)}), bf16[256,8192]{1,0:T(8,128)(2,1)}) %all-gather.5.cloned.1.call-update) | async-done | bytes 4194320 | tf_op jit(solution)/shard_map/all_gather | solution.py:254
  62.0 0.0 copy-start.5
  62.0 0.8 copy-done.5
  62.7 7.0 %project.1 = (bf16[64,64,128]{2,1,0:T(8,128)(2,1)S(1)}, bf16[64,64,128]{2,1,0:T(8,128)(2,1)}) custom-call(s32[64]{0:T(128)S(1)} %reshape.71.ids, bf16[64,256]{1,0:T(8,128)(2,1)S(1)} %bitcast.24, bf16[256,8192]{1,0:T(8,128)(2,1)} %all-gather.5.cloned.1.call-done.x_ref), custom_call_target="tpu_custom_call" | custom-call | flops 268435456 | bytes 12582912 | tf_op jit(solution)/shard_map/project/pallas_call | solution.py:46
  69.8 7.8 %all-to-all-start = ((bf16[64,64,128]{2,1,0:T(8,128)(2,1)}), bf16[64,64,128]{2,1,0:T(8,128)(2,1)S(1)}, u32[]{:S(2)}, u32[]{:S(2)}) async-start(bf16[64,64,128]{2,1,0:T(8,128)(2,1)} %get-tuple-element.12), calls=%async_computation | async-start | bytes 2097152 | tf_op jit(solution)/shard_map/all_to_all | solution.py:260
  77.6 0.0 copy-done.6
  77.7 0.0 copy-start.1
  77.7 14.2 %forward_local.1.acc_ref = f32[65,64,128]{2,1,0:T(8,128)S(1)} custom-call(s32[384]{0:T(512)S(1)} %get-tuple-element.26.src, s32[384]{0:T(512)S(1)} %get-tuple-element.25.dst, bf16[64,64,128]{2,1,0:T(8,128)(2,1)S(1)} %get-tuple-element.11.x_ref, bf16[384,128,128]{2,1,0:T(8,128)(2,1)} %tile_ref.3), custom_call_target="tpu_custom_call" | custom-call | flops 3221225472 | bytes 20971520 | tf_op jit(solution)/shard_map/forward_local/pallas_call | solution.py:91
  91.9 0.0 copy-start
  91.9 1.3 copy-done
  93.2 1.3 all-to-all-done.recv_ref
  94.5 0.0 copy-done.1
  94.5 9.7 %middle.1 = (bf16[64,8192]{1,0:T(8,128)(2,1)}, bf16[64,64,128]{2,1,0:T(8,128)(2,1)S(1)}, bf16[64,64,128]{2,1,0:T(8,128)(2,1)S(1)}) custom-call(s32[64]{0:T(128)S(1)} %broadcast_select_fusion.4.slots, s32[64]{0:T(128)S(1)} %broadcast_select_fusion.3.rows, f32[65,64,128]{2,1,0:T(8,128)} %copy-done, bf16[64,64,128]{2,1,0:T(8,128)(2,1)S(1)} %all-to-all-done.recv_ref, ...), custom_call_target="tpu_custom_call" | custom-call | tf_op jit(solution)/shard_map/middle/pallas_call | solution.py:163
  104.3 0.0 copy-start.2
  104.3 1.0 copy-done.2
  105.3 0.0 copy-start.4
  105.3 1.0 copy-done.4
  106.2 6.0 %all-to-all-start.1 = ((bf16[64,64,128]{2,1,0:T(8,128)(2,1)}), bf16[64,64,128]{2,1,0:T(8,128)(2,1)S(1)}, u32[]{:S(2)}, u32[]{:S(2)}) async-start(bf16[64,64,128]{2,1,0:T(8,128)(2,1)} %copy-done.4), calls=%async_computation.1 | async-start | bytes 2097152 | tf_op jit(solution)/shard_map/all_to_all | solution.py:263
  112.3 0.0 all-gather.7.cloned.1.call-start
  112.3 0.0 copy-start.3
  112.3 1.2 copy-done.3
  113.6 11.5 %backward_local.1.acc_ref = f32[65,64,128]{2,1,0:T(8,128)S(1)} custom-call(s32[384]{0:T(512)S(1)} %copy-done.6, s32[384]{0:T(512)S(1)} %get-tuple-element.21.dst, bf16[64,64,128]{2,1,0:T(8,128)(2,1)S(1)} %copy-done.3, bf16[384,128,128]{2,1,0:T(8,128)(2,1)} %tile_ref.3), custom_call_target="tpu_custom_call" | custom-call | flops 3221225472 | bytes 20971520 | tf_op jit(solution)/shard_map/backward_local/pallas_call | solution.py:91
  125.1 4.1 %all-to-all-done.1.recv_ref = bf16[64,64,128]{2,1,0:T(8,128)(2,1)S(1)} async-done(((bf16[64,64,128]{2,1,0:T(8,128)(2,1)}), bf16[64,64,128]{2,1,0:T(8,128)(2,1)S(1)}, u32[]{:S(2)}, u32[]{:S(2)}) %all-to-all-start.1) | async-done | bytes 1048608 | tf_op jit(solution)/shard_map/all_to_all | solution.py:263
  129.2 2.3 %finish.1 = bf16[64,8192]{1,0:T(8,128)(2,1)} custom-call(s32[64]{0:T(128)S(1)} %reshape.71.ids, f32[65,64,128]{2,1,0:T(8,128)S(1)} %backward_local.1.acc_ref, bf16[64,64,128]{2,1,0:T(8,128)(2,1)S(1)} %all-to-all-done.1.recv_ref), custom_call_target="tpu_custom_call" | custom-call | tf_op jit(solution)/shard_map/finish/pallas_call | solution.py:204
  131.4 0.0 all-gather.7.cloned.1.call-update
  131.5 3.9 %fusion.4 = f32[64,256]{1,0:T(8,128)S(1)} fusion(bf16[64,8192]{1,0:T(8,128)(2,1)} %finish.1, bf16[256,8192]{1,0:T(8,128)(2,1)} %all-gather.5.cloned.1.call-done.x_ref), kind=kOutput, calls=%fused_computation.32 | convolution fusion | flops 268435456 | bytes 5308416 | tf_op jit(solution)/shard_map/fn,kn->fk/dot_general | solution.py:267
  135.4 11.1 %all_to_all.15 = f32[32,4,128]{2,1,0:T(4,128)S(1)} all-to-all(f32[32,4,128]{2,1,0:T(4,128)S(1)} %reshape.72), channel_id=1, replica_groups=mesh['nodes'=32,'feat'=4] {'nodes'}, dimensions={0} | all-to-all | bytes 131072 | tf_op jit(solution)/shard_map/all_to_all | solution.py:269
  146.6 22.6 %all-gather.1 = f32[32,4,128]{2,1,0:T(4,128)S(1)} all-gather(f32[1,4,128]{2,1,0:T(4,128)S(1)} %multiply_bitcast_fusion), channel_id=1, replica_groups=mesh['nodes'=32,'feat'=4] {'nodes'}, dimensions={0}, use_global_device_ids=true | all-gather | bytes 67584 | tf_op jit(solution)/shard_map/all_gather | solution.py:271
  169.2 0.7 reshape.73
  169.8 6.4 %all-gather.7.cloned.1.call-done = bf16[256,8192]{1,0:T(8,128)(2,1)} async-done(((bf16[64,8192]{1,0:T(8,128)(2,1)}), bf16[256,8192]{1,0:T(8,128)(2,1)}) %all-gather.7.cloned.1.call-update) | async-done | bytes 4194320 | tf_op jit(solution)/shard_map/all_gather | solution.py:266
  176.3 4.1 %convolution_convert_fusion = bf16[8192,64]{0,1:T(8,128)(2,1)} fusion(bf16[256,8192]{1,0:T(8,128)(2,1)} %all-gather.7.cloned.1.call-done, bf16[256,64]{1,0:T(8,128)(2,1)S(1)} %constant_dynamic-slice_fusion), kind=kOutput, calls=%fused_computation | convolution fusion | flops 268959744 | bytes 5275648 | tf_op jit(solution)/shard_map/fk,fn->kn/dot_general | solution.py:272
  (11 shorter events, 0.1 us)
Async XLA Ops:
  7.2 70.5 %copy-start.6 = (s32[384]{0:T(512)S(1)}, s32[384]{0:T(512)}, u32[]{:S(2)}) copy-start(s32[384]{0:T(512)} %src.1) | copy-start | bytes 4612
  7.2 54.8 %all-gather.5.cloned.1.call-start = ((), (), s32[]{:S(2)}) async-start(), calls=%async_computation.3 | async-start | bytes 5242880 | tf_op jit(solution)/shard_map/all_gather | solution.py:254
  62.0 0.8 copy-start.5
  69.8 24.8 %all-to-all-start = ((bf16[64,64,128]{2,1,0:T(8,128)(2,1)}), bf16[64,64,128]{2,1,0:T(8,128)(2,1)S(1)}, u32[]{:S(2)}, u32[]{:S(2)}) async-start(bf16[64,64,128]{2,1,0:T(8,128)(2,1)} %get-tuple-element.12), calls=%async_computation | async-start | bytes 2097152 | tf_op jit(solution)/shard_map/all_to_all | solution.py:260
  77.7 16.9 %copy-start.1 = (bf16[8192,64]{0,1:T(8,128)(2,1)S(1)}, bf16[8192,64]{0,1:T(8,128)(2,1)}, u32[]{:S(2)}) copy-start(bf16[8192,64]{0,1:T(8,128)(2,1)} %param.11) | copy-start | bytes 3145732
  91.9 1.3 copy-start
  104.3 1.0 copy-start.2
  105.3 1.0 copy-start.4
  106.2 22.9 %all-to-all-start.1 = ((bf16[64,64,128]{2,1,0:T(8,128)(2,1)}), bf16[64,64,128]{2,1,0:T(8,128)(2,1)S(1)}, u32[]{:S(2)}, u32[]{:S(2)}) async-start(bf16[64,64,128]{2,1,0:T(8,128)(2,1)} %copy-done.4), calls=%async_computation.1 | async-start | bytes 2097152 | tf_op jit(solution)/shard_map/all_to_all | solution.py:263
  112.3 64.0 %all-gather.7.cloned.1.call-start = ((), (), s32[]{:S(2)}) async-start(), calls=%async_computation.4 | async-start | bytes 5242880 | tf_op jit(solution)/shard_map/all_gather | solution.py:266
  112.3 1.2 copy-start.3
Sparse Core Ops, SparseCore 0:
  9.6 52.2 all-gather.4
  131.6 44.6 all-gather.6
